TPU v7x, 128 devices: a whole 4x4x4 slice. The times are simulated.
128 devices in a mesh: chan: 2 (over x_hi), blk: 64 (over y, z, x_lo, core).
Axes of the slice: x: 4 (x_hi: 2, x_lo: 2; x = x_hi * 2 + x_lo), y: 4, z: 4, core: 2. Of those that a mesh axis runs over, the one named last changes fastest.
Arguments:
- features: bfloat16 [64, 2, 256, 128], P('blk', 'chan'), may hold values from -6 to 6
- transforms: bfloat16 [8, 128, 128], replicated, may hold values from -0.5 to 0.5
- self_weight: bfloat16 [128, 128], replicated, may hold values from -0.5 to 0.5
- tile_rows: int32 [8, 64, 64, 8], P('chan', 'blk'), may hold values from 0 to 3
- tile_cols: int32 [8, 64, 64, 8], P('chan', 'blk'), may hold values from 0 to 3
- tile_ids: int32 [8, 64, 64, 8], P('chan', 'blk'), may hold values from 0 to 31
- tile_count: int32 [8, 64, 64], P('chan', 'blk'), may hold values from 0 to 8
- tile_pool: bfloat16 [8, 64, 32, 128, 128], P('chan', 'blk'), may hold values from -0.0234375 to 0.0234375
Outputs:
- updated: bfloat16 [64, 2, 256, 128], P('blk', 'chan')
All inputs are finite; a program needn't handle non-finite values.
Results may differ from a plain program's by a relative error of at most 0.0041.
Values may be sent and summed in bfloat16 or wider, within the bound.
No kernel may reach another device: no remote copies, remote signals or barrier semaphores. Data moves between devices by JAX's collectives and lax.ppermute only.
A program may use at most 128 MiB of HBM per device.

v0:
```python
import math
import jax
import jax.numpy as jnp
from jax import lax
from jax.sharding import PartitionSpec as P


def shards(
    features, transforms, self_weight, tile_rows, tile_cols, tile_ids, tile_count, tile_pool
):
    chan_count = lax.axis_size("chan")
    chan_index = lax.axis_index("chan")
    own_rows = features[0, 0]
    half_rows = own_rows.shape[0]
    width = own_rows.shape[1]
    tile_size = tile_pool.shape[-1]
    pool_size = tile_pool.shape[2]
    block_rows = half_rows * chan_count
    tiles_block = block_rows // tile_size
    rel_dev = transforms.shape[0] // chan_count
    slot_count = tile_rows.shape[-1]
    rows_list = tile_rows[:, 0]
    cols_list = tile_cols[:, 0]
    ids_list = tile_ids[:, 0]
    count_list = tile_count[:, 0]
    pool_flat = tile_pool[:, 0].reshape(rel_dev, pool_size, tile_size * tile_size)
    slot_range = jnp.arange(slot_count)
    tile_range = jnp.arange(tiles_block)
    pool_range = jnp.arange(pool_size)

    def apply_group(total, hidden_group, first):
        group = hidden_group.shape[1]
        cols_now = lax.dynamic_slice_in_dim(cols_list, first, group, 1)
        rows_now = lax.dynamic_slice_in_dim(rows_list, first, group, 1)
        ids_now = lax.dynamic_slice_in_dim(ids_list, first, group, 1)
        count_now = lax.dynamic_slice_in_dim(count_list, first, group, 1)
        pick_cols = (cols_now[..., None] == tile_range).astype(jnp.bfloat16)
        flat_hidden = hidden_group.reshape(rel_dev, group, tiles_block, tile_size * width)
        picked = jnp.einsum(
            "rgks,rgsx->rgkx", pick_cols, flat_hidden, preferred_element_type=jnp.float32
        ).astype(jnp.bfloat16)
        picked = picked.reshape(rel_dev, group, slot_count, tile_size, width)
        pick_ids = (ids_now[..., None] == pool_range).astype(jnp.bfloat16)
        weights = jnp.einsum(
            "rgkp,rpx->rgkx", pick_ids, pool_flat, preferred_element_type=jnp.float32
        ).astype(jnp.bfloat16)
        weights = weights.reshape(rel_dev, group, slot_count, tile_size, tile_size)
        product = jnp.einsum(
            "rgkab,rgkbd->rgkad", weights, picked, preferred_element_type=jnp.float32
        )
        live = (slot_range < count_now[..., None]).astype(jnp.float32)
        onehot = (rows_now[..., None] == tile_range).astype(jnp.float32) * live[..., None]
        return total + jnp.einsum(
            "rgkt,rgkad->tad", onehot, product, precision=lax.Precision.HIGHEST
        )

    empty = jnp.zeros((tiles_block, tile_size, width), jnp.float32)
    all_hidden = jnp.einsum(
        "nd,rde->rne", own_rows, transforms, preferred_element_type=jnp.float32
    ).astype(jnp.bfloat16)
    mine = lax.all_to_all(all_hidden, "chan", split_axis=0, concat_axis=1, tiled=True)
    piece = lax.all_gather(mine, "blk", axis=1, tiled=True)
    blocks_here = piece.shape[1] // block_rows

    def fetch(offset, group):
        part_rows = lax.dynamic_slice_in_dim(piece, offset * block_rows, group * block_rows, 1)
        return part_rows.reshape(rel_dev, group, tiles_block, tile_size, width)

    group = math.gcd(blocks_here, 4)
    turns = blocks_here // group

    def step_once(turn, carry):
        return apply_group(carry, fetch(turn * group, group), turn * group)

    agg = lax.fori_loop(0, turns, step_once, empty)
    partial_rows = agg.reshape(block_rows, width)
    summed = lax.psum(partial_rows, "chan")
    share = lax.dynamic_slice_in_dim(summed, chan_index * half_rows, half_rows, 0)
    selfterm = jnp.dot(own_rows, self_weight, preferred_element_type=jnp.float32)
    updated = jax.nn.relu(selfterm + share).astype(jnp.bfloat16)
    return updated.reshape(1, 1, half_rows, width)


def solution(mesh):
    placed = (
        P("blk", "chan", None, None),
        P(),
        P(),
        P("chan", "blk", None, None),
        P("chan", "blk", None, None),
        P("chan", "blk", None, None),
        P("chan", "blk", None),
        P("chan", "blk", None, None, None),
    )
    return jax.shard_map(
        shards, mesh=mesh, in_specs=placed, out_specs=P("blk", "chan", None, None), check_vma=False
    )
```

profile of v0, /device:TPU:1, one launch (start us, length us, event | category | flops | bytes accessed | tf_op | source)
XLA Modules:
  0.0 706.5 jit_solution(2026471395278241592)
XLA Ops:
  8.7 13.2 %all_to_all.18 = bf16[8,256,128]{1,2,0:T(8,128)(2,1)S(1)} all-to-all(bf16[8,256,128]{1,2,0:T(8,128)(2,1)S(1)} %fusion.31), channel_id=1, replica_groups=mesh['chan'=2,'blk'=64] {'chan'}, dimensions={0} | all-to-all | bytes 1048576 | tf_op jit(solution)/shard_map/all_to_all | solution.py:61
  23.0 7.3 %reshape_squeeze.3 = bf16[4,32,16384]{2,1,0:T(8,128)(2,1)} reshape(bf16[4,1,32,128,128]{4,3,2,1,0:T(8,128)(2,1)} %param.17) | data formatting | bytes 8388608 | tf_op jit(solution)/shard_map/reshape;squeeze | solution.py:26
  30.8 181.1 %all-gather.2.cloned.1.call-done = bf16[4,32768,128]{2,1,0:T(8,128)(2,1)} async-done(((bf16[4,512,128]{2,1,0:T(8,128)(2,1)}), bf16[4,32768,128]{2,1,0:T(8,128)(2,1)}) %all-gather.2.cloned.1.call-update) | async-done | bytes 33554448 | tf_op jit(solution)/shard_map/all_gather | solution.py:62
  211.9 453.9 %while.17 = (s32[]{:T(128)}, f32[4,128,128]{2,0,1:T(4,128)S(1)}, s32[4,64,8]{2,0,1:T(4,128)S(1)}, s32[4,64]{0,1:T(8,128)S(1)}, s32[4,64,8]{2,1,0:T(8,128)S(1)}, ...) while((s32[]{:T(128)}, f32[4,128,128]{2,0,1:T(4,128)S(1)}, ...), condition=%wide.region_1.0_spmd.clone.clone, body=%wide.region_0.0_spmd.clone.clone.sunk | while | flops 792860416 | bytes 65542100 | solution.py:75
  221.1 4.5 fusion.61
  225.6 14.6 %fusion.63 = f32[4,128,128]{2,0,1:T(4,128)S(1)} fusion(f32[4,4,8,128,128]{4,3,2,1,0:T(8,128)} %fusion.61, f32[4,128,128]{2,0,1:T(4,128)S(1)} %get-tuple-element.418, pred[]{:T(512)S(6)} %compare.3, f32[4,4,8]{2,0,1:T(4,128)S(1)} %fusion.62, s32[4,4,8]{2,0,1:T(4,128)S(1)} %get-tuple-element.402), kind=kOutput, calls=%fused_computation.14.clone.1 | convolution fusion | flops 100795392 | bytes 8913921 | tf_op jit(solution)/shard_map/while/body/eval_jaxpr/rgkt,rgkad->tad/dot_general | solution.py:53
  249.4 4.5 fusion.61
  254.0 14.6 %fusion.63 = f32[4,128,128]{2,0,1:T(4,128)S(1)} fusion(f32[4,4,8,128,128]{4,3,2,1,0:T(8,128)} %fusion.61, f32[4,128,128]{2,0,1:T(4,128)S(1)} %get-tuple-element.418, pred[]{:T(512)S(6)} %compare.3, f32[4,4,8]{2,0,1:T(4,128)S(1)} %fusion.62, s32[4,4,8]{2,0,1:T(4,128)S(1)} %get-tuple-element.402), kind=kOutput, calls=%fused_computation.14.clone.1 | convolution fusion | flops 100795392 | bytes 8913921 | tf_op jit(solution)/shard_map/while/body/eval_jaxpr/rgkt,rgkad->tad/dot_general | solution.py:53
  282.3 14.6 %fusion.63 = f32[4,128,128]{2,0,1:T(4,128)S(1)} fusion(f32[4,4,8,128,128]{4,3,2,1,0:T(8,128)} %fusion.61, f32[4,128,128]{2,0,1:T(4,128)S(1)} %get-tuple-element.418, pred[]{:T(512)S(6)} %compare.3, f32[4,4,8]{2,0,1:T(4,128)S(1)} %fusion.62, s32[4,4,8]{2,0,1:T(4,128)S(1)} %get-tuple-element.402), kind=kOutput, calls=%fused_computation.14.clone.1 | convolution fusion | flops 100795392 | bytes 8913921 | tf_op jit(solution)/shard_map/while/body/eval_jaxpr/rgkt,rgkad->tad/dot_general | solution.py:53
  306.2 4.5 fusion.61
  310.7 14.6 %fusion.63 = f32[4,128,128]{2,0,1:T(4,128)S(1)} fusion(f32[4,4,8,128,128]{4,3,2,1,0:T(8,128)} %fusion.61, f32[4,128,128]{2,0,1:T(4,128)S(1)} %get-tuple-element.418, pred[]{:T(512)S(6)} %compare.3, f32[4,4,8]{2,0,1:T(4,128)S(1)} %fusion.62, s32[4,4,8]{2,0,1:T(4,128)S(1)} %get-tuple-element.402), kind=kOutput, calls=%fused_computation.14.clone.1 | convolution fusion | flops 100795392 | bytes 8913921 | tf_op jit(solution)/shard_map/while/body/eval_jaxpr/rgkt,rgkad->tad/dot_general | solution.py:53
  334.5 4.5 fusion.61
  339.1 14.6 %fusion.63 = f32[4,128,128]{2,0,1:T(4,128)S(1)} fusion(f32[4,4,8,128,128]{4,3,2,1,0:T(8,128)} %fusion.61, f32[4,128,128]{2,0,1:T(4,128)S(1)} %get-tuple-element.418, pred[]{:T(512)S(6)} %compare.3, f32[4,4,8]{2,0,1:T(4,128)S(1)} %fusion.62, s32[4,4,8]{2,0,1:T(4,128)S(1)} %get-tuple-element.402), kind=kOutput, calls=%fused_computation.14.clone.1 | convolution fusion | flops 100795392 | bytes 8913921 | tf_op jit(solution)/shard_map/while/body/eval_jaxpr/rgkt,rgkad->tad/dot_general | solution.py:53
  367.5 14.6 %fusion.63 = f32[4,128,128]{2,0,1:T(4,128)S(1)} fusion(f32[4,4,8,128,128]{4,3,2,1,0:T(8,128)} %fusion.61, f32[4,128,128]{2,0,1:T(4,128)S(1)} %get-tuple-element.418, pred[]{:T(512)S(6)} %compare.3, f32[4,4,8]{2,0,1:T(4,128)S(1)} %fusion.62, s32[4,4,8]{2,0,1:T(4,128)S(1)} %get-tuple-element.402), kind=kOutput, calls=%fused_computation.14.clone.1 | convolution fusion | flops 100795392 | bytes 8913921 | tf_op jit(solution)/shard_map/while/body/eval_jaxpr/rgkt,rgkad->tad/dot_general | solution.py:53
  391.3 4.5 fusion.61
  395.8 14.6 %fusion.63 = f32[4,128,128]{2,0,1:T(4,128)S(1)} fusion(f32[4,4,8,128,128]{4,3,2,1,0:T(8,128)} %fusion.61, f32[4,128,128]{2,0,1:T(4,128)S(1)} %get-tuple-element.418, pred[]{:T(512)S(6)} %compare.3, f32[4,4,8]{2,0,1:T(4,128)S(1)} %fusion.62, s32[4,4,8]{2,0,1:T(4,128)S(1)} %get-tuple-element.402), kind=kOutput, calls=%fused_computation.14.clone.1 | convolution fusion | flops 100795392 | bytes 8913921 | tf_op jit(solution)/shard_map/while/body/eval_jaxpr/rgkt,rgkad->tad/dot_general | solution.py:53
  419.7 4.5 fusion.61
  424.2 14.6 %fusion.63 = f32[4,128,128]{2,0,1:T(4,128)S(1)} fusion(f32[4,4,8,128,128]{4,3,2,1,0:T(8,128)} %fusion.61, f32[4,128,128]{2,0,1:T(4,128)S(1)} %get-tuple-element.418, pred[]{:T(512)S(6)} %compare.3, f32[4,4,8]{2,0,1:T(4,128)S(1)} %fusion.62, s32[4,4,8]{2,0,1:T(4,128)S(1)} %get-tuple-element.402), kind=kOutput, calls=%fused_computation.14.clone.1 | convolution fusion | flops 100795392 | bytes 8913921 | tf_op jit(solution)/shard_map/while/body/eval_jaxpr/rgkt,rgkad->tad/dot_general | solution.py:53
  452.6 14.6 %fusion.63 = f32[4,128,128]{2,0,1:T(4,128)S(1)} fusion(f32[4,4,8,128,128]{4,3,2,1,0:T(8,128)} %fusion.61, f32[4,128,128]{2,0,1:T(4,128)S(1)} %get-tuple-element.418, pred[]{:T(512)S(6)} %compare.3, f32[4,4,8]{2,0,1:T(4,128)S(1)} %fusion.62, s32[4,4,8]{2,0,1:T(4,128)S(1)} %get-tuple-element.402), kind=kOutput, calls=%fused_computation.14.clone.1 | convolution fusion | flops 100795392 | bytes 8913921 | tf_op jit(solution)/shard_map/while/body/eval_jaxpr/rgkt,rgkad->tad/dot_general | solution.py:53
  476.4 4.5 fusion.61
  480.9 14.6 %fusion.63 = f32[4,128,128]{2,0,1:T(4,128)S(1)} fusion(f32[4,4,8,128,128]{4,3,2,1,0:T(8,128)} %fusion.61, f32[4,128,128]{2,0,1:T(4,128)S(1)} %get-tuple-element.418, pred[]{:T(512)S(6)} %compare.3, f32[4,4,8]{2,0,1:T(4,128)S(1)} %fusion.62, s32[4,4,8]{2,0,1:T(4,128)S(1)} %get-tuple-element.402), kind=kOutput, calls=%fused_computation.14.clone.1 | convolution fusion | flops 100795392 | bytes 8913921 | tf_op jit(solution)/shard_map/while/body/eval_jaxpr/rgkt,rgkad->tad/dot_general | solution.py:53
  504.8 4.5 fusion.61
  509.3 14.6 %fusion.63 = f32[4,128,128]{2,0,1:T(4,128)S(1)} fusion(f32[4,4,8,128,128]{4,3,2,1,0:T(8,128)} %fusion.61, f32[4,128,128]{2,0,1:T(4,128)S(1)} %get-tuple-element.418, pred[]{:T(512)S(6)} %compare.3, f32[4,4,8]{2,0,1:T(4,128)S(1)} %fusion.62, s32[4,4,8]{2,0,1:T(4,128)S(1)} %get-tuple-element.402), kind=kOutput, calls=%fused_computation.14.clone.1 | convolution fusion | flops 100795392 | bytes 8913921 | tf_op jit(solution)/shard_map/while/body/eval_jaxpr/rgkt,rgkad->tad/dot_general | solution.py:53
  537.7 14.6 %fusion.63 = f32[4,128,128]{2,0,1:T(4,128)S(1)} fusion(f32[4,4,8,128,128]{4,3,2,1,0:T(8,128)} %fusion.61, f32[4,128,128]{2,0,1:T(4,128)S(1)} %get-tuple-element.418, pred[]{:T(512)S(6)} %compare.3, f32[4,4,8]{2,0,1:T(4,128)S(1)} %fusion.62, s32[4,4,8]{2,0,1:T(4,128)S(1)} %get-tuple-element.402), kind=kOutput, calls=%fused_computation.14.clone.1 | convolution fusion | flops 100795392 | bytes 8913921 | tf_op jit(solution)/shard_map/while/body/eval_jaxpr/rgkt,rgkad->tad/dot_general | solution.py:53
  561.5 4.5 fusion.61
  566.0 14.6 %fusion.63 = f32[4,128,128]{2,0,1:T(4,128)S(1)} fusion(f32[4,4,8,128,128]{4,3,2,1,0:T(8,128)} %fusion.61, f32[4,128,128]{2,0,1:T(4,128)S(1)} %get-tuple-element.418, pred[]{:T(512)S(6)} %compare.3, f32[4,4,8]{2,0,1:T(4,128)S(1)} %fusion.62, s32[4,4,8]{2,0,1:T(4,128)S(1)} %get-tuple-element.402), kind=kOutput, calls=%fused_computation.14.clone.1 | convolution fusion | flops 100795392 | bytes 8913921 | tf_op jit(solution)/shard_map/while/body/eval_jaxpr/rgkt,rgkad->tad/dot_general | solution.py:53
  589.9 4.5 fusion.61
  594.4 14.6 %fusion.63 = f32[4,128,128]{2,0,1:T(4,128)S(1)} fusion(f32[4,4,8,128,128]{4,3,2,1,0:T(8,128)} %fusion.61, f32[4,128,128]{2,0,1:T(4,128)S(1)} %get-tuple-element.418, pred[]{:T(512)S(6)} %compare.3, f32[4,4,8]{2,0,1:T(4,128)S(1)} %fusion.62, s32[4,4,8]{2,0,1:T(4,128)S(1)} %get-tuple-element.402), kind=kOutput, calls=%fused_computation.14.clone.1 | convolution fusion | flops 100795392 | bytes 8913921 | tf_op jit(solution)/shard_map/while/body/eval_jaxpr/rgkt,rgkad->tad/dot_general | solution.py:53
  622.8 14.6 %fusion.63 = f32[4,128,128]{2,0,1:T(4,128)S(1)} fusion(f32[4,4,8,128,128]{4,3,2,1,0:T(8,128)} %fusion.61, f32[4,128,128]{2,0,1:T(4,128)S(1)} %get-tuple-element.418, pred[]{:T(512)S(6)} %compare.3, f32[4,4,8]{2,0,1:T(4,128)S(1)} %fusion.62, s32[4,4,8]{2,0,1:T(4,128)S(1)} %get-tuple-element.402), kind=kOutput, calls=%fused_computation.14.clone.1 | convolution fusion | flops 100795392 | bytes 8913921 | tf_op jit(solution)/shard_map/while/body/eval_jaxpr/rgkt,rgkad->tad/dot_general | solution.py:53
  646.6 4.5 fusion.61
  651.2 14.6 %fusion.63 = f32[4,128,128]{2,0,1:T(4,128)S(1)} fusion(f32[4,4,8,128,128]{4,3,2,1,0:T(8,128)} %fusion.61, f32[4,128,128]{2,0,1:T(4,128)S(1)} %get-tuple-element.418, pred[]{:T(512)S(6)} %compare.3, f32[4,4,8]{2,0,1:T(4,128)S(1)} %fusion.62, s32[4,4,8]{2,0,1:T(4,128)S(1)} %get-tuple-element.402), kind=kOutput, calls=%fused_computation.14.clone.1 | convolution fusion | flops 100795392 | bytes 8913921 | tf_op jit(solution)/shard_map/while/body/eval_jaxpr/rgkt,rgkad->tad/dot_general | solution.py:53
  666.5 31.5 %all-reduce.2.cloned.1.call-done = f32[512,128]{1,0:T(8,128)} async-done(((f32[512,128]{1,0:T(8,128)}), f32[512,128]{1,0:T(8,128)}) %all-reduce.2.cloned.1.call-update) | async-done | bytes 262160 | tf_op jit(solution)/shard_map/psum | solution.py:77
  (192 shorter events, 176.1 us)
Async XLA Ops:
  6.5 1.0 copy-start
  6.5 205.3 %all-gather.2.cloned.1.call-start = ((), (), s32[]{:S(2)}) async-start(), calls=%async_computation.1 | async-start | bytes 34078720 | tf_op jit(solution)/shard_map/all_gather | solution.py:62
  22.9 675.1 %all-reduce.2.cloned.1.call-start = ((), (), s32[]{:S(2)}) async-start(), calls=%async_computation.2 | async-start | bytes 524288 | tf_op jit(solution)/shard_map/psum | solution.py:77
  22.9 7.4 %copy-start.4 = (s32[4,1,64,8]{2,3,1,0:T(8,128)S(1)}, s32[4,1,64,8]{2,3,1,0:T(8,128)}, u32[]{:S(2)}) copy-start(s32[4,1,64,8]{2,3,1,0:T(8,128)} %param.13) | copy-start | bytes 24580
  23.0 7.5 %copy-start.5 = (s32[4,1,64,8]{2,3,1,0:T(8,128)S(1)}, s32[4,1,64,8]{2,3,1,0:T(8,128)}, u32[]{:S(2)}) copy-start(s32[4,1,64,8]{2,3,1,0:T(8,128)} %param.15) | copy-start | bytes 24580
  23.0 7.6 %copy-start.6 = (s32[4,1,64,8]{2,3,1,0:T(8,128)S(1)}, s32[4,1,64,8]{2,3,1,0:T(8,128)}, u32[]{:S(2)}) copy-start(s32[4,1,64,8]{2,3,1,0:T(8,128)} %param.14) | copy-start | bytes 24580
  23.0 7.7 %copy-start.7 = (s32[4,1,64]{2,1,0:T(1,128)S(1)}, s32[4,1,64]{2,1,0:T(1,128)}, u32[]{:S(2)}) copy-start(s32[4,1,64]{2,1,0:T(1,128)} %param.16) | copy-start | bytes 3076
  211.8 486.1 %copy-start.2 = (bf16[1,1,256,128]{3,2,1,0:T(8,128)(2,1)S(1)}, bf16[1,1,256,128]{3,2,1,0:T(8,128)(2,1)}, u32[]{:S(2)}) copy-start(bf16[1,1,256,128]{3,2,1,0:T(8,128)(2,1)} %param.10) | copy-start | bytes 196612
  211.9 486.1 %copy-start.3 = (bf16[128,128]{1,0:T(8,128)(2,1)S(1)}, bf16[128,128]{1,0:T(8,128)(2,1)}, u32[]{:S(2)}) copy-start(bf16[128,128]{1,0:T(8,128)(2,1)} %param.12) | copy-start | bytes 98308
  217.6 2.2 copy-start.1
  245.9 2.2 copy-start.1
  274.3 2.2 copy-start.1
  302.7 2.2 copy-start.1
  331.1 2.2 copy-start.1
  359.4 2.2 copy-start.1
  387.8 2.2 copy-start.1
  416.2 2.2 copy-start.1
  444.5 2.2 copy-start.1
  472.9 2.2 copy-start.1
  501.3 2.2 copy-start.1
  529.6 2.2 copy-start.1
  558.0 2.2 copy-start.1
  586.4 2.2 copy-start.1
  614.8 2.2 copy-start.1
  643.1 2.2 copy-start.1
Sparse Core Ops, SparseCore 0:
  23.0 188.7 all-gather.1
  666.6 31.2 all-reduce.1
where the time goes:
time: 709 us; the launch traced here: 706 us
  matrix products  357 us (50%)
  waiting for transfers between devices  213 us (30%)
  local copies, waits for them, and re-layouts  108 us (15%)
  between operations  13.5 us (2%)
  blocking collectives  13.2 us (2%)
    dot_general x16, matrix products, apply_group(): jnp.einsum('rgkt,rgkad->tad', onehot, product, precision=lax.Precision.HI...  233 us
    all_gather x1, waiting for transfers between devices, shards(): piece = lax.all_gather(mine, 'blk', axis=1, tiled=True)  181 us
    dot_general x16, matrix products, apply_group(): jnp.einsum('rgkab,rgkbd->rgkad', weights, picked, preferred_element_type=...  71.4 us
    dynamic_slice x16, local copies, waits for them, and re-layouts, fetch(): lax.dynamic_slice_in_dim(piece, offset * block_rows, group * block_rows, 1)  49 us
    reshape x16, local copies, waits for them, and re-layouts, apply_group(): hidden_group.reshape(rel_dev, group, tiles_block, tile_size * width)  42 us
    psum x1, waiting for transfers between devices, shards(): summed = lax.psum(partial_rows, 'chan')  31.5 us
    dot_general x16, matrix products, apply_group(): jnp.einsum('rgks,rgsx->rgkx', pick_cols, flat_hidden, preferred_element_t...  28.2 us
    dot_general x16, matrix products, apply_group(): jnp.einsum('rgkp,rpx->rgkx', pick_ids, pool_flat, preferred_element_type=...  20.7 us
  transfers between devices with their start and end apart: 2, of which 2 were waited for; matrix products, arithmetic and copies ran while one was open for 1% of the time, Pallas kernels for 0%

commit v1 on v0

--- a/solution.py
+++ b/solution.py
@@ -59,7 +59,10 @@
         "nd,rde->rne", own_rows, transforms, preferred_element_type=jnp.float32
     ).astype(jnp.bfloat16)
     mine = lax.all_to_all(all_hidden, "chan", split_axis=0, concat_axis=1, tiled=True)
-    piece = lax.all_gather(mine, "blk", axis=1, tiled=True)
+    size = lax.axis_size("blk")
+    tiles = jnp.stack([mine for _ in range(size)])
+    tiles = lax.all_to_all(tiles, "blk", split_axis=0, concat_axis=0)
+    piece = jnp.concatenate(tiles, axis=1)
     blocks_here = piece.shape[1] // block_rows
 
     def fetch(offset, group):

time: 709 us -> 1070 us (1.51)
  waiting for transfers between devices: 213 us -> 531 us
  local copies, waits for them, and re-layouts: 108 us -> 142 us
    all_to_all x0 -> x1, waiting for transfers between devices: none -> 430 us  [shards(): tiles = lax.all_to_all(tiles, 'blk', split_axis=0, concat_axis=0)]
    all_gather x1 -> x0, waiting for transfers between devices: 181 us -> none  [shards(): piece = lax.all_gather(mine, 'blk', axis=1, tiled=True)]
    psum x1, waiting for transfers between devices: 31.5 us -> 100 us  [shards(): summed = lax.psum(partial_rows, 'chan')]
    all_to_all x0 -> x1, local copies, waits for them, and re-layouts: none -> 23 us  [shards(): tiles = lax.all_to_all(tiles, 'blk', split_axis=0, concat_axis=0)]
    another operation x0 -> x1, local copies, waits for them, and re-layouts: none -> 11.3 us  [shards(): tiles = jnp.stack([mine for _ in range(size)])]
where the time goes in v1:
time: 1070 us
  waiting for transfers between devices  531 us (50%)
  matrix products  357 us (33%)
  local copies, waits for them, and re-layouts  142 us (13%)
  between operations  13.5 us (1%)
  blocking collectives  13.2 us (1%)
    all_to_all x1, waiting for transfers between devices, shards(): tiles = lax.all_to_all(tiles, 'blk', split_axis=0, concat_axis=0)  430 us
    dot_general x16, matrix products, apply_group(): jnp.einsum('rgkt,rgkad->tad', onehot, product, precision=lax.Precision.HI...  233 us
    psum x1, waiting for transfers between devices, shards(): summed = lax.psum(partial_rows, 'chan')  100 us
    dot_general x16, matrix products, apply_group(): jnp.einsum('rgkab,rgkbd->rgkad', weights, picked, preferred_element_type=...  71.4 us
    dynamic_slice x16, local copies, waits for them, and re-layouts, fetch(): lax.dynamic_slice_in_dim(piece, offset * block_rows, group * block_rows, 1)  49 us
    reshape x16, local copies, waits for them, and re-layouts, apply_group(): hidden_group.reshape(rel_dev, group, tiles_block, tile_size * width)  42 us
    dot_general x16, matrix products, apply_group(): jnp.einsum('rgks,rgsx->rgkx', pick_cols, flat_hidden, preferred_element_t...  28.2 us
    all_to_all x1, local copies, waits for them, and re-layouts, shards(): tiles = lax.all_to_all(tiles, 'blk', split_axis=0, concat_axis=0)  23 us
  transfers between devices with their start and end apart: 2, of which 2 were waited for; matrix products, arithmetic and copies ran while one was open for 1% of the time, Pallas kernels for 0%

profile of v1, /device:TPU:1, one launch (start us, length us, event | category | flops | bytes accessed | tf_op | source)
XLA Modules:
  0.0 1068.8 jit_solution(7793653117662679595)
XLA Ops:
  8.7 13.2 %all_to_all.20 = bf16[8,256,128]{1,2,0:T(8,128)(2,1)S(1)} all-to-all(bf16[8,256,128]{1,2,0:T(8,128)(2,1)S(1)} %fusion.31), channel_id=1, replica_groups=mesh['chan'=2,'blk'=64] {'chan'}, dimensions={0} | all-to-all | bytes 1048576 | tf_op jit(solution)/shard_map/all_to_all | solution.py:61
  22.1 11.3 %stack.5 = bf16[64,4,512,128]{3,2,1,0:T(8,128)(2,1)} broadcast(bf16[4,512,128]{2,1,0:T(8,128)(2,1)S(1)} %bitcast.63), dimensions={1,2,3} | broadcast | bytes 34078720 | tf_op jit(solution)/shard_map/stack | solution.py:63
  33.5 10.6 all-to-all-start.1
  44.2 7.3 reshape_squeeze.3
  52.0 430.4 %all-to-all-done.1 = bf16[64,4,512,128]{3,2,1,0:T(8,128)(2,1)} async-done(((bf16[64,4,512,128]{3,2,1,0:T(8,128)(2,1)}), bf16[64,4,512,128]{3,2,1,0:T(8,128)(2,1)}, u32[]{:S(2)}, u32[]{:S(2)}) %all-to-all-start.1) | async-done | bytes 33554464 | tf_op jit(solution)/shard_map/all_to_all | solution.py:64
  482.4 23.0 %copy.45 = bf16[64,4,512,128]{3,2,0,1:T(8,128)(2,1)} copy(bf16[64,4,512,128]{3,2,1,0:T(8,128)(2,1)} %all-to-all-done.1) | data formatting | bytes 67108864 | tf_op jit(solution)/shard_map/all_to_all | solution.py:64
  505.4 453.9 %while.17 = (s32[]{:T(128)}, f32[4,128,128]{2,0,1:T(4,128)S(1)}, s32[4,64,8]{2,0,1:T(4,128)S(1)}, s32[4,64]{0,1:T(8,128)S(1)}, s32[4,64,8]{2,1,0:T(8,128)S(1)}, ...) while((s32[]{:T(128)}, f32[4,128,128]{2,0,1:T(4,128)S(1)}, ...), condition=%wide.region_1.0_spmd.clone.clone, body=%wide.region_0.0_spmd.clone.clone.sunk | while | flops 792860416 | bytes 65542100 | solution.py:78
  514.6 4.5 fusion.61
  519.1 14.6 %fusion.63 = f32[4,128,128]{2,0,1:T(4,128)S(1)} fusion(f32[4,4,8,128,128]{4,3,2,1,0:T(8,128)} %fusion.61, f32[4,128,128]{2,0,1:T(4,128)S(1)} %get-tuple-element.418, pred[]{:T(512)S(6)} %compare.3, f32[4,4,8]{2,0,1:T(4,128)S(1)} %fusion.62, s32[4,4,8]{2,0,1:T(4,128)S(1)} %get-tuple-element.402), kind=kOutput, calls=%fused_computation.14.clone.1 | convolution fusion | flops 100795392 | bytes 8913921 | tf_op jit(solution)/shard_map/while/body/eval_jaxpr/rgkt,rgkad->tad/dot_general | solution.py:53
  542.9 4.5 fusion.61
  547.5 14.6 %fusion.63 = f32[4,128,128]{2,0,1:T(4,128)S(1)} fusion(f32[4,4,8,128,128]{4,3,2,1,0:T(8,128)} %fusion.61, f32[4,128,128]{2,0,1:T(4,128)S(1)} %get-tuple-element.418, pred[]{:T(512)S(6)} %compare.3, f32[4,4,8]{2,0,1:T(4,128)S(1)} %fusion.62, s32[4,4,8]{2,0,1:T(4,128)S(1)} %get-tuple-element.402), kind=kOutput, calls=%fused_computation.14.clone.1 | convolution fusion | flops 100795392 | bytes 8913921 | tf_op jit(solution)/shard_map/while/body/eval_jaxpr/rgkt,rgkad->tad/dot_general | solution.py:53
  575.9 14.6 %fusion.63 = f32[4,128,128]{2,0,1:T(4,128)S(1)} fusion(f32[4,4,8,128,128]{4,3,2,1,0:T(8,128)} %fusion.61, f32[4,128,128]{2,0,1:T(4,128)S(1)} %get-tuple-element.418, pred[]{:T(512)S(6)} %compare.3, f32[4,4,8]{2,0,1:T(4,128)S(1)} %fusion.62, s32[4,4,8]{2,0,1:T(4,128)S(1)} %get-tuple-element.402), kind=kOutput, calls=%fused_computation.14.clone.1 | convolution fusion | flops 100795392 | bytes 8913921 | tf_op jit(solution)/shard_map/while/body/eval_jaxpr/rgkt,rgkad->tad/dot_general | solution.py:53
  599.7 4.5 fusion.61
  604.2 14.6 %fusion.63 = f32[4,128,128]{2,0,1:T(4,128)S(1)} fusion(f32[4,4,8,128,128]{4,3,2,1,0:T(8,128)} %fusion.61, f32[4,128,128]{2,0,1:T(4,128)S(1)} %get-tuple-element.418, pred[]{:T(512)S(6)} %compare.3, f32[4,4,8]{2,0,1:T(4,128)S(1)} %fusion.62, s32[4,4,8]{2,0,1:T(4,128)S(1)} %get-tuple-element.402), kind=kOutput, calls=%fused_computation.14.clone.1 | convolution fusion | flops 100795392 | bytes 8913921 | tf_op jit(solution)/shard_map/while/body/eval_jaxpr/rgkt,rgkad->tad/dot_general | solution.py:53
  628.1 4.5 fusion.61
  632.6 14.6 %fusion.63 = f32[4,128,128]{2,0,1:T(4,128)S(1)} fusion(f32[4,4,8,128,128]{4,3,2,1,0:T(8,128)} %fusion.61, f32[4,128,128]{2,0,1:T(4,128)S(1)} %get-tuple-element.418, pred[]{:T(512)S(6)} %compare.3, f32[4,4,8]{2,0,1:T(4,128)S(1)} %fusion.62, s32[4,4,8]{2,0,1:T(4,128)S(1)} %get-tuple-element.402), kind=kOutput, calls=%fused_computation.14.clone.1 | convolution fusion | flops 100795392 | bytes 8913921 | tf_op jit(solution)/shard_map/while/body/eval_jaxpr/rgkt,rgkad->tad/dot_general | solution.py:53
  661.0 14.6 %fusion.63 = f32[4,128,128]{2,0,1:T(4,128)S(1)} fusion(f32[4,4,8,128,128]{4,3,2,1,0:T(8,128)} %fusion.61, f32[4,128,128]{2,0,1:T(4,128)S(1)} %get-tuple-element.418, pred[]{:T(512)S(6)} %compare.3, f32[4,4,8]{2,0,1:T(4,128)S(1)} %fusion.62, s32[4,4,8]{2,0,1:T(4,128)S(1)} %get-tuple-element.402), kind=kOutput, calls=%fused_computation.14.clone.1 | convolution fusion | flops 100795392 | bytes 8913921 | tf_op jit(solution)/shard_map/while/body/eval_jaxpr/rgkt,rgkad->tad/dot_general | solution.py:53
  684.8 4.5 fusion.61
  689.3 14.6 %fusion.63 = f32[4,128,128]{2,0,1:T(4,128)S(1)} fusion(f32[4,4,8,128,128]{4,3,2,1,0:T(8,128)} %fusion.61, f32[4,128,128]{2,0,1:T(4,128)S(1)} %get-tuple-element.418, pred[]{:T(512)S(6)} %compare.3, f32[4,4,8]{2,0,1:T(4,128)S(1)} %fusion.62, s32[4,4,8]{2,0,1:T(4,128)S(1)} %get-tuple-element.402), kind=kOutput, calls=%fused_computation.14.clone.1 | convolution fusion | flops 100795392 | bytes 8913921 | tf_op jit(solution)/shard_map/while/body/eval_jaxpr/rgkt,rgkad->tad/dot_general | solution.py:53
  717.7 14.6 %fusion.63 = f32[4,128,128]{2,0,1:T(4,128)S(1)} fusion(f32[4,4,8,128,128]{4,3,2,1,0:T(8,128)} %fusion.61, f32[4,128,128]{2,0,1:T(4,128)S(1)} %get-tuple-element.418, pred[]{:T(512)S(6)} %compare.3, f32[4,4,8]{2,0,1:T(4,128)S(1)} %fusion.62, s32[4,4,8]{2,0,1:T(4,128)S(1)} %get-tuple-element.402), kind=kOutput, calls=%fused_computation.14.clone.1 | convolution fusion | flops 100795392 | bytes 8913921 | tf_op jit(solution)/shard_map/while/body/eval_jaxpr/rgkt,rgkad->tad/dot_general | solution.py:53
  746.1 14.6 %fusion.63 = f32[4,128,128]{2,0,1:T(4,128)S(1)} fusion(f32[4,4,8,128,128]{4,3,2,1,0:T(8,128)} %fusion.61, f32[4,128,128]{2,0,1:T(4,128)S(1)} %get-tuple-element.418, pred[]{:T(512)S(6)} %compare.3, f32[4,4,8]{2,0,1:T(4,128)S(1)} %fusion.62, s32[4,4,8]{2,0,1:T(4,128)S(1)} %get-tuple-element.402), kind=kOutput, calls=%fused_computation.14.clone.1 | convolution fusion | flops 100795392 | bytes 8913921 | tf_op jit(solution)/shard_map/while/body/eval_jaxpr/rgkt,rgkad->tad/dot_general | solution.py:53
  769.9 4.5 fusion.61
  774.5 14.6 %fusion.63 = f32[4,128,128]{2,0,1:T(4,128)S(1)} fusion(f32[4,4,8,128,128]{4,3,2,1,0:T(8,128)} %fusion.61, f32[4,128,128]{2,0,1:T(4,128)S(1)} %get-tuple-element.418, pred[]{:T(512)S(6)} %compare.3, f32[4,4,8]{2,0,1:T(4,128)S(1)} %fusion.62, s32[4,4,8]{2,0,1:T(4,128)S(1)} %get-tuple-element.402), kind=kOutput, calls=%fused_computation.14.clone.1 | convolution fusion | flops 100795392 | bytes 8913921 | tf_op jit(solution)/shard_map/while/body/eval_jaxpr/rgkt,rgkad->tad/dot_general | solution.py:53
  802.8 14.6 %fusion.63 = f32[4,128,128]{2,0,1:T(4,128)S(1)} fusion(f32[4,4,8,128,128]{4,3,2,1,0:T(8,128)} %fusion.61, f32[4,128,128]{2,0,1:T(4,128)S(1)} %get-tuple-element.418, pred[]{:T(512)S(6)} %compare.3, f32[4,4,8]{2,0,1:T(4,128)S(1)} %fusion.62, s32[4,4,8]{2,0,1:T(4,128)S(1)} %get-tuple-element.402), kind=kOutput, calls=%fused_computation.14.clone.1 | convolution fusion | flops 100795392 | bytes 8913921 | tf_op jit(solution)/shard_map/while/body/eval_jaxpr/rgkt,rgkad->tad/dot_general | solution.py:53
  831.2 14.6 %fusion.63 = f32[4,128,128]{2,0,1:T(4,128)S(1)} fusion(f32[4,4,8,128,128]{4,3,2,1,0:T(8,128)} %fusion.61, f32[4,128,128]{2,0,1:T(4,128)S(1)} %get-tuple-element.418, pred[]{:T(512)S(6)} %compare.3, f32[4,4,8]{2,0,1:T(4,128)S(1)} %fusion.62, s32[4,4,8]{2,0,1:T(4,128)S(1)} %get-tuple-element.402), kind=kOutput, calls=%fused_computation.14.clone.1 | convolution fusion | flops 100795392 | bytes 8913921 | tf_op jit(solution)/shard_map/while/body/eval_jaxpr/rgkt,rgkad->tad/dot_general | solution.py:53
  855.0 4.5 fusion.61
  859.6 14.6 %fusion.63 = f32[4,128,128]{2,0,1:T(4,128)S(1)} fusion(f32[4,4,8,128,128]{4,3,2,1,0:T(8,128)} %fusion.61, f32[4,128,128]{2,0,1:T(4,128)S(1)} %get-tuple-element.418, pred[]{:T(512)S(6)} %compare.3, f32[4,4,8]{2,0,1:T(4,128)S(1)} %fusion.62, s32[4,4,8]{2,0,1:T(4,128)S(1)} %get-tuple-element.402), kind=kOutput, calls=%fused_computation.14.clone.1 | convolution fusion | flops 100795392 | bytes 8913921 | tf_op jit(solution)/shard_map/while/body/eval_jaxpr/rgkt,rgkad->tad/dot_general | solution.py:53
  887.9 14.6 %fusion.63 = f32[4,128,128]{2,0,1:T(4,128)S(1)} fusion(f32[4,4,8,128,128]{4,3,2,1,0:T(8,128)} %fusion.61, f32[4,128,128]{2,0,1:T(4,128)S(1)} %get-tuple-element.418, pred[]{:T(512)S(6)} %compare.3, f32[4,4,8]{2,0,1:T(4,128)S(1)} %fusion.62, s32[4,4,8]{2,0,1:T(4,128)S(1)} %get-tuple-element.402), kind=kOutput, calls=%fused_computation.14.clone.1 | convolution fusion | flops 100795392 | bytes 8913921 | tf_op jit(solution)/shard_map/while/body/eval_jaxpr/rgkt,rgkad->tad/dot_general | solution.py:53
  916.3 14.6 %fusion.63 = f32[4,128,128]{2,0,1:T(4,128)S(1)} fusion(f32[4,4,8,128,128]{4,3,2,1,0:T(8,128)} %fusion.61, f32[4,128,128]{2,0,1:T(4,128)S(1)} %get-tuple-element.418, pred[]{:T(512)S(6)} %compare.3, f32[4,4,8]{2,0,1:T(4,128)S(1)} %fusion.62, s32[4,4,8]{2,0,1:T(4,128)S(1)} %get-tuple-element.402), kind=kOutput, calls=%fused_computation.14.clone.1 | convolution fusion | flops 100795392 | bytes 8913921 | tf_op jit(solution)/shard_map/while/body/eval_jaxpr/rgkt,rgkad->tad/dot_general | solution.py:53
  940.1 4.5 fusion.61
  944.7 14.6 %fusion.63 = f32[4,128,128]{2,0,1:T(4,128)S(1)} fusion(f32[4,4,8,128,128]{4,3,2,1,0:T(8,128)} %fusion.61, f32[4,128,128]{2,0,1:T(4,128)S(1)} %get-tuple-element.418, pred[]{:T(512)S(6)} %compare.3, f32[4,4,8]{2,0,1:T(4,128)S(1)} %fusion.62, s32[4,4,8]{2,0,1:T(4,128)S(1)} %get-tuple-element.402), kind=kOutput, calls=%fused_computation.14.clone.1 | convolution fusion | flops 100795392 | bytes 8913921 | tf_op jit(solution)/shard_map/while/body/eval_jaxpr/rgkt,rgkad->tad/dot_general | solution.py:53
  960.0 100.3 %all-reduce.2.cloned.1.call-done = f32[512,128]{1,0:T(8,128)} async-done(((f32[512,128]{1,0:T(8,128)}), f32[512,128]{1,0:T(8,128)}) %all-reduce.2.cloned.1.call-update) | async-done | bytes 262160 | tf_op jit(solution)/shard_map/psum | solution.py:80
  (195 shorter events, 188.7 us)
Async XLA Ops:
  6.5 1.0 copy-start
  33.5 448.9 %all-to-all-start.1 = ((bf16[64,4,512,128]{3,2,1,0:T(8,128)(2,1)}), bf16[64,4,512,128]{3,2,1,0:T(8,128)(2,1)}, u32[]{:S(2)}, u32[]{:S(2)}) async-start(bf16[64,4,512,128]{3,2,1,0:T(8,128)(2,1)} %stack.5), calls=%async_computation.1 | async-start | bytes 67108864 | tf_op jit(solution)/shard_map/all_to_all | solution.py:64
  44.1 1016.2 %all-reduce.2.cloned.1.call-start = ((), (), s32[]{:S(2)}) async-start(), calls=%async_computation.2 | async-start | bytes 524288 | tf_op jit(solution)/shard_map/psum | solution.py:80
  44.1 7.4 copy-start.5
  44.1 7.5 copy-start.6
  44.1 7.6 copy-start.7
  44.2 7.7 copy-start.8
  505.3 555.0 %copy-start.3 = (bf16[1,1,256,128]{3,2,1,0:T(8,128)(2,1)S(1)}, bf16[1,1,256,128]{3,2,1,0:T(8,128)(2,1)}, u32[]{:S(2)}) copy-start(bf16[1,1,256,128]{3,2,1,0:T(8,128)(2,1)} %param.10) | copy-start | bytes 196612
  505.3 555.0 %copy-start.4 = (bf16[128,128]{1,0:T(8,128)(2,1)S(1)}, bf16[128,128]{1,0:T(8,128)(2,1)}, u32[]{:S(2)}) copy-start(bf16[128,128]{1,0:T(8,128)(2,1)} %param.12) | copy-start | bytes 98308
  511.1 2.2 copy-start.2
  539.5 2.2 copy-start.2
  567.8 2.2 copy-start.2
  596.2 2.2 copy-start.2
  624.6 2.2 copy-start.2
  652.9 2.2 copy-start.2
  681.3 2.2 copy-start.2
  709.7 2.2 copy-start.2
  738.1 2.2 copy-start.2
  766.4 2.2 copy-start.2
  794.8 2.2 copy-start.2
  823.2 2.2 copy-start.2
  851.5 2.2 copy-start.2
  879.9 2.2 copy-start.2
  908.3 2.2 copy-start.2
  936.6 2.2 copy-start.2
  959.3 102.7 %copy-start.1 = (bf16[8,128,128]{2,1,0:T(8,128)(2,1)S(1)}, bf16[8,128,128]{2,1,0:T(8,128)(2,1)}, u32[]{:S(2)}) copy-start(bf16[8,128,128]{2,1,0:T(8,128)(2,1)} %param.11) | copy-start | bytes 786436
Sparse Core Ops, SparseCore 0:
  960.2 100.0 all-reduce.1
